TPU v7x, 128 devices: a whole 4x4x4 slice. The times are simulated.
128 devices in a mesh: ctx: 16 (over y, x), exp: 8 (over z, core).
Axes of the slice: x: 4, y: 4, z: 4, core: 2. Of those that a mesh axis runs over, the one named last changes fastest.
Arguments:
- queries: bfloat16 [4, 1024, 8192], P(None, 'ctx', 'exp'), may hold values from -2 to 2
- keys: bfloat16 [4, 1024, 8192], P(None, 'ctx', 'exp'), may hold values from -2 to 2
- values: bfloat16 [4, 1024, 8192], P(None, 'ctx', 'exp'), may hold values from -6 to 6
- decay_log: float32 [1024, 64], P('ctx', 'exp'), may hold values from -0.9 to 0
- out_gate: bfloat16 [4, 1024, 8192], P(None, 'ctx', 'exp'), may hold values from -6 to 6
- head_gain: float32 [8192], P('exp'), may hold values from 0.1 to 1.9
- out_weight: bfloat16 [8192, 6144], P('exp', 'ctx'), may hold values from -0.0625 to 0.0625
- stream: bfloat16 [4, 1024, 6144], P(None, ('ctx', 'exp')), may hold values from -6 to 6
- norm_gain: float32 [6144], replicated, may hold values from 0.1 to 1.9
- expert_ids: int32 [128, 32, 2], P(('ctx', 'exp')), may hold values from 0 to 7, all different within a row; in each aligned block of 32 rows (0 to 31, 32 to 63, ..., all dimensions but the last counted through in order) at most 9 rows name the same one
- expert_share: float32 [128, 32, 2], P(('ctx', 'exp')), may hold values from 0.2 to 1
- w_gate: bfloat16 [8, 6144, 9216], P('exp', None, 'ctx'), may hold values from -0.078125 to 0.078125
- w_up: bfloat16 [8, 6144, 9216], P('exp', None, 'ctx'), may hold values from -0.078125 to 0.078125
- w_down: bfloat16 [8, 9216, 6144], P('exp', 'ctx'), may hold values from -0.0625 to 0.0625
Outputs:
- layer_out: bfloat16 [4, 1024, 6144], P(None, ('ctx', 'exp'))
Inputs may be any that keep to these rules, and one draw needn't show every extreme that they name: `expert_ids`: within a routing group no expert takes more than 9 copies, some group gives one expert exactly 9, and the two picks of a token differ.
All inputs are finite; a program needn't handle non-finite values.
Results may differ from a plain program's by a relative error of at most 0.02.
Values may be sent and summed in bfloat16 or wider, within the bound.
A program may use at most 192 MiB of HBM per device.

v0:
```python
import jax
import jax.numpy as jnp
from jax import lax
from jax.sharding import PartitionSpec as P


def carried_in(x, axis, join, neutral):
    place = lax.axis_index(axis)
    gathered = jax.tree.map(
        lambda a, kind: lax.all_gather(a.astype(kind), axis), x, (jnp.bfloat16, jnp.bfloat16)
    )
    state = jax.tree.map(lambda a, e: jnp.zeros_like(a) + jnp.asarray(e, a.dtype), x, neutral)

    def one(lap, state):
        return join(
            state,
            jax.tree.map(
                lambda a, own: lax.dynamic_index_in_dim(a, lap, 0, False).astype(own.dtype),
                gathered,
                x,
            ),
        )

    return lax.fori_loop(0, place, one, state)


def join_states(earlier, later):
    earlier_fade, earlier_state = earlier
    later_fade, later_state = later
    return (earlier_fade * later_fade, later_fade * earlier_state + later_state)


def body(
    queries,
    keys,
    values,
    decay_log,
    out_gate,
    head_gain,
    out_weight,
    stream,
    norm_gain,
    expert_ids,
    expert_share,
    w_gate,
    w_up,
    w_down,
):
    seq_count, block_len, head_width = queries.shape
    head_count = decay_log.shape[1]
    head_dim = head_width // head_count
    split_shape = (seq_count, block_len, head_count, head_dim)
    query_heads = queries.reshape(split_shape)
    key_heads = keys.reshape(split_shape)
    value_heads = values.reshape(split_shape)
    cumulative = jnp.cumsum(decay_log, axis=0)
    position = jnp.arange(block_len)
    causal = position[:, None] >= position[None, :]
    gap_log = cumulative[:, None, :] - cumulative[None, :, :]
    decay_grid = jnp.exp(jnp.where(causal[:, :, None], gap_log, -1e30))
    scores = jnp.einsum(
        "sihd,sjhd->sijh", query_heads, key_heads, preferred_element_type=jnp.float32
    )
    weights = (scores * decay_grid[None]).astype(jnp.bfloat16)
    within = jnp.einsum("sijh,sjhd->sihd", weights, value_heads, preferred_element_type=jnp.float32)
    block_end = cumulative[-1]
    keys_faded = jnp.exp(block_end[None, :] - cumulative)[None, :, :, None] * key_heads.astype(
        jnp.float32
    )
    local_state = jnp.einsum(
        "sjhd,sjhe->shde",
        keys_faded,
        value_heads.astype(jnp.float32),
        precision=lax.Precision.HIGHEST,
    )
    fading = jnp.broadcast_to(
        jnp.exp(block_end)[None, :, None, None], (seq_count, head_count, 1, 1)
    )
    identity = (jnp.ones_like(fading), jnp.zeros_like(local_state))
    incoming_fade, incoming = carried_in((fading, local_state), "ctx", join_states, identity)
    carried = jnp.exp(cumulative)[None, :, :, None] * jnp.einsum(
        "sihd,shde->sihe",
        query_heads.astype(jnp.float32),
        incoming,
        precision=lax.Precision.HIGHEST,
    )
    attended = within + carried
    mean_square = jnp.mean(attended * attended, axis=-1, keepdims=True)
    gate_act = jax.nn.sigmoid(out_gate.reshape(split_shape).astype(jnp.float32))
    gated = (
        attended
        * lax.rsqrt(mean_square + 1e-06)
        * head_gain.reshape(head_count, head_dim)
        * gate_act
    )
    mixed = gated.astype(jnp.bfloat16).reshape(seq_count, block_len, head_width)
    sub_len = stream.shape[1]
    model_width = stream.shape[2]
    exp_count = lax.axis_size("exp")
    tok_count = seq_count * sub_len
    ordered = (
        mixed.reshape(seq_count, exp_count, sub_len, head_width)
        .transpose(1, 0, 2, 3)
        .reshape(exp_count * tok_count, head_width)
    )
    full_weight = lax.all_gather(out_weight, "ctx", axis=1, tiled=True)
    chosen_rows = ordered
    projected = lax.psum_scatter(
        jnp.dot(chosen_rows, full_weight, preferred_element_type=jnp.float32).astype(jnp.bfloat16),
        "exp",
        scatter_dimension=0,
        tiled=True,
    ).astype(jnp.float32)
    residual_sum = stream.reshape(tok_count, model_width).astype(jnp.float32) + projected
    stream_square = jnp.mean(residual_sum * residual_sum, axis=-1, keepdims=True)
    normed = (residual_sum * lax.rsqrt(stream_square + 1e-06) * norm_gain).astype(jnp.bfloat16)
    expert_local = w_gate.shape[0]
    expert_count = expert_local * exp_count
    capacity = max(2, (2 * tok_count + expert_count - 1) // expert_count + 1)
    slot_total = expert_count * capacity
    picks = expert_ids.reshape(2 * tok_count)
    one_hot = (picks[:, None] == jnp.arange(expert_count, dtype=jnp.int32)[None, :]).astype(
        jnp.int32
    )
    ranking = jnp.sum(jnp.cumsum(one_hot, axis=0) * one_hot, axis=1) - 1
    slot_of = picks * capacity + ranking
    placing = slot_of[:, None] == jnp.arange(slot_total, dtype=jnp.int32)[None, :]
    copies = jnp.repeat(normed, 2, axis=0)
    dispatch = jnp.dot(
        placing.T.astype(jnp.bfloat16), copies, preferred_element_type=jnp.float32
    ).astype(jnp.bfloat16)
    dispatch = dispatch.reshape(exp_count, expert_local, capacity, model_width)
    received = lax.all_to_all(dispatch, "exp", split_axis=0, concat_axis=0, tiled=True)
    piece = lax.all_gather(received, "ctx", axis=0, tiled=True)
    gate_part = jnp.einsum("nemd,edh->nemh", piece, w_gate, preferred_element_type=jnp.float32)
    up_part = jnp.einsum("nemd,edh->nemh", piece, w_up, preferred_element_type=jnp.float32)
    hidden_units = (jax.nn.silu(gate_part) * up_part).astype(jnp.bfloat16)
    chosen_rows = hidden_units
    summed = lax.psum_scatter(
        jnp.einsum(
            "nemh,ehd->nemd", chosen_rows, w_down, preferred_element_type=jnp.float32
        ).astype(jnp.bfloat16),
        "ctx",
        scatter_dimension=0,
        tiled=True,
    )
    returned = lax.all_to_all(summed, "exp", split_axis=0, concat_axis=0, tiled=True).reshape(
        slot_total, model_width
    )
    weighting = jnp.where(placing, expert_share.reshape(2 * tok_count, 1), 0.0)
    weighting = jnp.sum(weighting.reshape(tok_count, 2, slot_total), axis=1)
    expert_mix = jnp.dot(weighting, returned.astype(jnp.float32), precision=lax.Precision.HIGHEST)
    result = (residual_sum + expert_mix).astype(jnp.bfloat16)
    return result.reshape(seq_count, sub_len, model_width)


def solution(mesh):
    return jax.shard_map(
        body,
        mesh=mesh,
        in_specs=(
            P(None, "ctx", "exp"),
            P(None, "ctx", "exp"),
            P(None, "ctx", "exp"),
            P("ctx", "exp"),
            P(None, "ctx", "exp"),
            P("exp"),
            P("exp", "ctx"),
            P(None, ("ctx", "exp"), None),
            P(),
            P(("ctx", "exp"), None, None),
            P(("ctx", "exp"), None, None),
            P("exp", None, "ctx"),
            P("exp", None, "ctx"),
            P("exp", "ctx", None),
        ),
        out_specs=P(None, ("ctx", "exp"), None),
        check_vma=False,
    )
```

profile of v0, /device:TPU:1, one launch (start us, length us, event | category | flops | bytes accessed | tf_op | source)
XLA Modules:
  0.0 671.2 jit_solution(6845622781889080944)
XLA Ops:
  6.5 0.8 copy.71
  7.4 0.1 reduce_window_sum.22
  7.6 4.0 convolution_convert_fusion.2
  11.7 0.7 all-gather.6.cloned.1.call-update
  12.5 0.7 fusion.50
  13.9 0.2 dynamic-update-slice
  14.1 34.7 %all-reduce = bf16[128]{0:T(256)(128)(2,1)S(1)} all-reduce(bf16[128]{0:T(256)(128)(2,1)S(1)} %dynamic-update-slice), channel_id=3, replica_groups=mesh['ctx'=16,'exp'=8] {'ctx'}, use_global_device_ids=true, to_apply=%add | all-reduce | flops 128 | bytes 512
  48.8 0.1 reshape.188
  49.0 0.1 select_exponential_fusion
  49.2 77.1 %all-gather.10.cloned.1.call-done = bf16[64,8,128,128]{3,2,1,0:T(8,128)(2,1)} async-done(((bf16[4,8,128,128]{3,2,1,0:T(8,128)(2,1)}), bf16[64,8,128,128]{3,2,1,0:T(8,128)(2,1)}) %all-gather.10.cloned.1.call-update) | async-done | bytes 16777232 | tf_op jit(solution)/shard_map/all_gather | solution.py:10
  126.3 0.2 broadcast_in_dim.28
  126.5 3.2 fusion.24
  129.7 2.3 multiply_reduce_fusion
  132.0 0.4 fusion.26
  132.4 0.3 copy.82
  132.7 0.2 reshape_reshape.3
  133.0 93.8 %all-gather.6.cloned.1.call-done = bf16[1024,6144]{1,0:T(8,128)(2,1)} async-done(((bf16[1024,384]{1,0:T(8,128)(2,1)}), bf16[1024,6144]{1,0:T(8,128)(2,1)}) %all-gather.6.cloned.1.call-update) | async-done | bytes 12582928 | tf_op jit(solution)/shard_map/all_gather | solution.py:106
  226.8 9.4 %convolution_convert_fusion = bf16[256,6144]{1,0:T(8,128)(2,1)} fusion(bf16[256,1024]{1,0:T(8,128)(2,1)S(1)} %bitcast.180, bf16[1024,6144]{1,0:T(8,128)(2,1)} %all-gather.6.cloned.1.call-done), kind=kOutput, calls=%fused_computation.7 | convolution fusion | flops 3222798336 | bytes 16252928 | tf_op jit(solution)/shard_map/dot_general | solution.py:109
  236.3 0.6 copy-done.7
  236.9 0.1 copy.84
  236.9 0.1 eq.35
  237.0 0.1 fusion.47
  237.1 0.1 reduce_window_sum.23
  237.2 0.2 select_reduce_fusion.1
  237.4 31.9 %reduce-scatter.3.cloned.1.call-done = bf16[32,6144]{1,0:T(8,128)(2,1)} async-done(((bf16[256,6144]{1,0:T(8,128)(2,1)}), bf16[32,6144]{1,0:T(8,128)(2,1)}) %reduce-scatter.3.cloned.1.call-update) | async-done | bytes 393232 | tf_op jit(solution)/shard_map/reduce_scatter | solution.py:108
  269.4 1.2 multiply_reduce_fusion.1
  270.6 1.1 multiply_convert_fusion
  271.8 0.5 broadcast_in_dim.32
  272.2 0.3 reshape.172
  272.5 0.5 convolution_convert_fusion.1
  273.0 0.4 reshape.173
  273.5 27.1 %all_to_all.10 = bf16[8,1,9,6144]{3,2,1,0:T(8,128)(2,1)S(1)} all-to-all(bf16[8,1,9,6144]{3,2,1,0:T(8,128)(2,1)S(1)} %bitcast.177), channel_id=1, replica_groups=mesh['ctx'=16,'exp'=8] {'exp'}, dimensions={0} | all-to-all | bytes 1769472 | tf_op jit(solution)/shard_map/all_to_all | solution.py:133
  300.6 1.5 copy.87
  302.1 0.2 all-reduce.4.cloned.1.call-start
  302.3 97.3 %all-gather.8.cloned.1.call-done = bf16[128,1,9,6144]{3,0,2,1:T(8,128)(2,1)} async-done(((bf16[8,1,9,6144]{3,0,2,1:T(8,128)(2,1)}), bf16[128,1,9,6144]{3,0,2,1:T(8,128)(2,1)}) %all-gather.8.cloned.1.call-update) | async-done | bytes 14155792 | tf_op jit(solution)/shard_map/all_gather | solution.py:134
  399.6 13.7 %fusion = f32[128,9,576]{0,2,1:T(8,128)S(1)} fusion(bf16[128,1,9,6144]{3,0,2,1:T(8,128)(2,1)} %all-gather.8.cloned.1.call-done, bf16[1,6144,576]{1,2,0:T(8,128)(2,1)} %param.28), kind=kOutput, calls=%fused_computation.2 | convolution fusion | flops 8153726976 | bytes 23887872 | tf_op jit(solution)/shard_map/nemd,edh->nemh/dot_general | solution.py:136
  413.4 12.1 %fusion.17 = bf16[128,9,576]{0,2,1:T(8,128)(2,1)S(1)} fusion(f32[128,9,576]{0,2,1:T(8,128)S(1)} %fusion, bf16[1,6144,576]{1,2,0:T(8,128)(2,1)} %param.27, bf16[128,1,9,6144]{3,0,2,1:T(8,128)(2,1)S(1)} %copy-done.10), kind=kOutput, calls=%fused_computation.23 | convolution fusion | flops 8157708288 | bytes 25214976 | tf_op jit(solution)/shard_map/nemd,edh->nemh/dot_general | solution.py:135
  425.5 14.1 %convert_bitcast_fusion = bf16[128,1,9,6144]{3,0,2,1:T(8,128)(2,1)} fusion(bf16[128,9,576]{0,2,1:T(8,128)(2,1)S(1)} %fusion.17, bf16[1,576,6144]{2,1,0:T(8,128)(2,1)S(1)} %bitcast.184), kind=kOutput, calls=%fused_computation.6 | convolution fusion | flops 8160804864 | bytes 22560768 | tf_op jit(solution)/shard_map/nemh,ehd->nemd/dot_general | solution.py:140
  440.3 192.9 %all-reduce.4.cloned.1.call-done = bf16[128,1,9,6144]{3,0,2,1:T(8,128)(2,1)} async-done(((bf16[128,1,9,6144]{3,0,2,1:T(8,128)(2,1)}), bf16[128,1,9,6144]{3,0,2,1:T(8,128)(2,1)}) %all-reduce.4.cloned.1.call-update) | async-done | bytes 14155792
  633.2 1.2 constant_dynamic-slice_fusion
  634.4 1.7 copy.88
  636.1 5.1 all-to-all-start.1
  641.2 0.1 sub.41
  641.3 0.1 copy.85
  641.4 0.1 select_reduce_fusion
  641.5 20.4 %all-to-all-done.1 = bf16[8,1,9,6144]{3,2,1,0:T(8,128)(2,1)S(1)} async-done(((bf16[8,1,9,6144]{3,2,1,0:T(8,128)(2,1)}), bf16[8,1,9,6144]{3,2,1,0:T(8,128)(2,1)S(1)}, u32[]{:S(2)}, u32[]{:S(2)}) %all-to-all-start.1) | async-done | bytes 884768 | tf_op jit(solution)/shard_map/all_to_all | solution.py:147
  661.9 0.4 reshape.179
  662.4 2.3 fusion.8
  (49 shorter events, 0.6 us)
Async XLA Ops:
  6.5 1.1 copy-start
  6.5 6.0 copy-start.8
  6.5 119.7 %all-gather.10.cloned.1.call-start = ((), (), s32[]{:S(2)}) async-start(), calls=%async_computation.6 | async-start | bytes 17825792 | tf_op jit(solution)/shard_map/all_gather | solution.py:10
  11.6 215.2 %all-gather.6.cloned.1.call-start = ((), (), s32[]{:S(2)}) async-start(), calls=%async_computation.3 | async-start | bytes 13369344 | tf_op jit(solution)/shard_map/all_gather | solution.py:106
  12.4 257.0 %reduce-scatter.3.cloned.1.call-start = ((), (), s32[]{:S(2)}) async-start(), calls=%async_computation.4 | async-start | bytes 3538944 | tf_op jit(solution)/shard_map/reduce_scatter | solution.py:108
  126.5 3.2 copy-start.3
  129.7 2.3 copy-start.4
  129.7 2.3 copy-start.6
  236.2 0.7 copy-start.7
  236.2 33.2 %copy-start.2 = (bf16[4,8,6144]{2,1,0:T(8,128)(2,1)S(1)}, bf16[4,8,6144]{2,1,0:T(8,128)(2,1)}, u32[]{:S(2)}) copy-start(bf16[4,8,6144]{2,1,0:T(8,128)(2,1)} %param.23) | copy-start | bytes 1179652
  236.2 34.4 %copy-start.5 = (f32[6144]{0:T(1024)S(1)}, f32[6144]{0:T(1024)}, u32[]{:S(2)}) copy-start(f32[6144]{0:T(1024)} %param.24) | copy-start | bytes 73732
  236.2 163.4 %all-gather.8.cloned.1.call-start = ((), (), s32[]{:S(2)}) async-start(), calls=%async_computation.5 | async-start | bytes 15040512 | tf_op jit(solution)/shard_map/all_gather | solution.py:134
  302.1 331.1 %all-reduce.4.cloned.1.call-start = ((), (), s32[]{:S(2)}) async-start(), calls=%async_computation.7 | async-start | bytes 28311552
  399.6 13.7 %copy-start.10 = (bf16[128,1,9,6144]{3,0,2,1:T(8,128)(2,1)S(1)}, bf16[128,1,9,6144]{3,0,2,1:T(8,128)(2,1)}, u32[]{:S(2)}) copy-start(bf16[128,1,9,6144]{3,0,2,1:T(8,128)(2,1)} %all-gather.8.cloned.1.call-done) | copy-start | bytes 42467332
  399.6 25.9 %slice-start = ((s8[7077888]{0:T(1024)(128)(4,1)}), s8[4194304]{0:T(1024)(128)(4,1)S(1)}, s32[]{:S(2)}) async-start(s8[7077888]{0:T(1024)(128)(4,1)} %bitcast.183), calls=%async_computation.8 | async-start | bytes 8388608
  413.4 12.1 %slice-start.1 = ((s8[7077888]{0:T(1024)(128)(4,1)}), s8[2883584]{0:T(1024)(128)(4,1)S(1)}, s32[]{:S(2)}) async-start(s8[7077888]{0:T(1024)(128)(4,1)} %bitcast.183), calls=%async_computation.9 | async-start | bytes 5767168
  634.4 7.0 %copy-start.9 = (f32[1,32,2]{1,2,0:T(2,128)S(1)}, f32[1,32,2]{1,2,0:T(2,128)}, u32[]{:S(2)}) copy-start(f32[1,32,2]{1,2,0:T(2,128)} %param.26) | copy-start | bytes 772
  636.1 25.8 %all-to-all-start.1 = ((bf16[8,1,9,6144]{3,2,1,0:T(8,128)(2,1)}), bf16[8,1,9,6144]{3,2,1,0:T(8,128)(2,1)S(1)}, u32[]{:S(2)}, u32[]{:S(2)}) async-start(bf16[8,1,9,6144]{3,2,1,0:T(8,128)(2,1)} %copy.88), calls=%async_computation.2 | async-start | bytes 3145728 | tf_op jit(solution)/shard_map/all_to_all | solution.py:147
  641.2 23.4 %copy-start.1 = (bf16[4,64,1024]{2,1,0:T(8,128)(2,1)S(1)}, bf16[4,64,1024]{2,1,0:T(8,128)(2,1)}, u32[]{:S(2)}) copy-start(bf16[4,64,1024]{2,1,0:T(8,128)(2,1)} %param.18) | copy-start | bytes 1572868
Sparse Core Ops, SparseCore 0:
  11.7 114.4 all-gather.9
  128.4 98.3 all-gather.5
  236.3 32.9 reduce-scatter.2
  302.2 97.3 all-gather.7
  439.8 193.3 all-reduce.3
where the time goes:
time: 672 us; the launch traced here: 671 us
  waiting for transfers between devices  514 us (76%)
  blocking collectives  61.9 us (9%)
  matrix products  61.5 us (9%)
  between operations  14.8 us (2%)
  local copies, waits for them, and re-layouts  9.89 us (1%)
    unnamed x6, waiting for transfers between devices  194 us
    all_gather x1, waiting for transfers between devices, body(): piece = lax.all_gather(received, 'ctx', axis=0, tiled=True)  97.3 us
    all_gather x1, waiting for transfers between devices, body(): full_weight = lax.all_gather(out_weight, 'ctx', axis=1, tiled=True)  93.8 us
    all_gather x1, waiting for transfers between devices, carried_in(): lax.all_gather(a.astype(kind), axis)  77.1 us
    unnamed x1, blocking collectives  34.7 us
    reduce_scatter x1, waiting for transfers between devices, body(): lax.psum_scatter(jnp.dot(chosen_rows, full_weight, preferred_element_type...  31.9 us
    all_to_all x1, blocking collectives, body(): lax.all_to_all(dispatch, 'exp', split_axis=0, concat_axis=0, tiled=True)  27.1 us
    all_to_all x1, waiting for transfers between devices, body(): lax.all_to_all(summed, 'exp', split_axis=0, concat_axis=0, tiled=True)  20.4 us
  transfers between devices with their start and end apart: 6, of which 6 were waited for; matrix products, arithmetic and copies ran while one was open for 1% of the time, Pallas kernels for 0%

commit v1 on v0

--- a/solution.py
+++ b/solution.py
@@ -131,7 +131,9 @@
     ).astype(jnp.bfloat16)
     dispatch = dispatch.reshape(exp_count, expert_local, capacity, model_width)
     received = lax.all_to_all(dispatch, "exp", split_axis=0, concat_axis=0, tiled=True)
-    piece = lax.all_gather(received, "ctx", axis=0, tiled=True)
+    piece = jnp.concatenate(
+        lax.all_to_all(jnp.stack([received] * lax.axis_size("ctx")), "ctx", 0, 0), axis=0
+    )
     gate_part = jnp.einsum("nemd,edh->nemh", piece, w_gate, preferred_element_type=jnp.float32)
     up_part = jnp.einsum("nemd,edh->nemh", piece, w_up, preferred_element_type=jnp.float32)
     hidden_units = (jax.nn.silu(gate_part) * up_part).astype(jnp.bfloat16)

time: 672 us -> 755 us (1.12)
  blocking collectives: 61.9 us -> 225 us
  waiting for transfers between devices: 514 us -> 413 us
  local copies, waits for them, and re-layouts: 9.89 us -> 21 us
  matrix products: 61.5 us -> 70.9 us
    all_to_all x0 -> x1, blocking collectives: none -> 163 us  [body(): lax.all_to_all(jnp.stack([received] * lax.axis_size('ctx')), 'ctx', 0, 0)]
    all_gather x1 -> x0, waiting for transfers between devices: 97.3 us -> none  [body(): piece = lax.all_gather(received, 'ctx', axis=0, tiled=True)]
    dot_general x1, matrix products: 14.1 us -> 32.2 us  [body(): jnp.einsum('nemh,ehd->nemd', chosen_rows, w_down, preferred_element_type=...]
    dot_general x1 -> x0, matrix products: 12.1 us -> none  [body(): jnp.einsum('nemd,edh->nemh', piece, w_gate, preferred_element_type=jnp.fl...]
    unnamed x6 -> x5, waiting for transfers between devices: 194 us -> 191 us
  transfers between devices with their start and end apart: 6 -> 5, of which waited for: 6 -> 5; matrix products, arithmetic and copies ran while one was open for 1% -> 1% of each run, Pallas kernels for 0% -> 0%
where the time goes in v1:
time: 755 us; the launch traced here: 754 us
  waiting for transfers between devices  413 us (55%)
  blocking collectives  225 us (30%)
  matrix products  70.9 us (9%)
  local copies, waits for them, and re-layouts  21 us (3%)
  between operations  14.8 us (2%)
    unnamed x5, waiting for transfers between devices  191 us
    all_to_all x1, blocking collectives, body(): lax.all_to_all(jnp.stack([received] * lax.axis_size('ctx')), 'ctx', 0, 0)  163 us
    all_gather x1, waiting for transfers between devices, body(): full_weight = lax.all_gather(out_weight, 'ctx', axis=1, tiled=True)  92.8 us
    all_gather x1, waiting for transfers between devices, carried_in(): lax.all_gather(a.astype(kind), axis)  76.3 us
    unnamed x1, blocking collectives  34.7 us
    reduce_scatter x1, waiting for transfers between devices, body(): lax.psum_scatter(jnp.dot(chosen_rows, full_weight, preferred_element_type...  32.5 us
    dot_general x1, matrix products, body(): jnp.einsum('nemh,ehd->nemd', chosen_rows, w_down, preferred_element_type=...  32.2 us
    all_to_all x1, blocking collectives, body(): lax.all_to_all(dispatch, 'exp', split_axis=0, concat_axis=0, tiled=True)  27.1 us
  transfers between devices with their start and end apart: 5, of which 5 were waited for; matrix products, arithmetic and copies ran while one was open for 1% of the time, Pallas kernels for 0%

profile of v1, /device:TPU:1, one launch (start us, length us, event | category | flops | bytes accessed | tf_op | source)
XLA Modules:
  0.0 754.2 jit_solution(11211776098043050935)
XLA Ops:
  6.5 0.8 copy.72
  7.4 0.1 reduce_window_sum.22
  7.6 4.0 convolution_convert_fusion.2
  11.7 0.7 all-gather.5.cloned.1.call-update
  12.4 0.1 copy.73
  12.5 1.4 fusion.58
  14.6 0.2 dynamic-update-slice
  14.8 34.7 %all-reduce = bf16[128]{0:T(256)(128)(2,1)S(1)} all-reduce(bf16[128]{0:T(256)(128)(2,1)S(1)} %dynamic-update-slice), channel_id=3, replica_groups=mesh['ctx'=16,'exp'=8] {'ctx'}, use_global_device_ids=true, to_apply=%add | all-reduce | flops 128 | bytes 512
  49.5 0.1 reshape.194
  49.7 0.1 select_exponential_fusion
  49.9 76.3 %all-gather.7.cloned.1.call-done = bf16[64,8,128,128]{3,2,1,0:T(8,128)(2,1)} async-done(((bf16[4,8,128,128]{3,2,1,0:T(8,128)(2,1)}), bf16[64,8,128,128]{3,2,1,0:T(8,128)(2,1)}) %all-gather.7.cloned.1.call-update) | async-done | bytes 16777232 | tf_op jit(solution)/shard_map/all_gather | solution.py:10
  126.2 0.2 broadcast_in_dim.28
  126.5 3.2 fusion.30
  129.7 2.2 multiply_reduce_fusion
  131.9 1.4 fusion.33
  133.3 0.3 copy.83
  133.7 0.2 reshape_reshape.3
  133.9 92.8 %all-gather.5.cloned.1.call-done = bf16[1024,6144]{1,0:T(8,128)(2,1)} async-done(((bf16[1024,384]{1,0:T(8,128)(2,1)}), bf16[1024,6144]{1,0:T(8,128)(2,1)}) %all-gather.5.cloned.1.call-update) | async-done | bytes 12582928 | tf_op jit(solution)/shard_map/all_gather | solution.py:106
  226.7 9.4 %convolution_convert_fusion = bf16[256,6144]{1,0:T(8,128)(2,1)} fusion(bf16[256,1024]{1,0:T(8,128)(2,1)S(1)} %bitcast.191, bf16[1024,6144]{1,0:T(8,128)(2,1)} %all-gather.5.cloned.1.call-done), kind=kOutput, calls=%fused_computation.9 | convolution fusion | flops 3222798336 | bytes 16252928 | tf_op jit(solution)/shard_map/dot_general | solution.py:109
  236.2 0.1 copy.85
  236.3 0.1 eq.35
  236.4 0.1 fusion.54
  236.5 0.1 reduce_window_sum.23
  236.6 0.2 select_reduce_fusion.1
  236.8 32.5 %reduce-scatter.3.cloned.1.call-done = bf16[32,6144]{1,0:T(8,128)(2,1)} async-done(((bf16[256,6144]{1,0:T(8,128)(2,1)}), bf16[32,6144]{1,0:T(8,128)(2,1)}) %reduce-scatter.3.cloned.1.call-update) | async-done | bytes 393232 | tf_op jit(solution)/shard_map/reduce_scatter | solution.py:108
  269.3 1.2 multiply_reduce_fusion.1
  270.6 1.2 multiply_convert_fusion
  271.7 0.5 broadcast_in_dim.32
  272.2 0.3 reshape.178
  272.5 0.5 convolution_convert_fusion.1
  273.0 0.4 reshape.179
  273.4 27.1 %all_to_all.18 = bf16[8,1,9,6144]{3,2,1,0:T(8,128)(2,1)S(1)} all-to-all(bf16[8,1,9,6144]{3,2,1,0:T(8,128)(2,1)S(1)} %bitcast.187), channel_id=1, replica_groups=mesh['ctx'=16,'exp'=8] {'exp'}, dimensions={0} | all-to-all | bytes 1769472 | tf_op jit(solution)/shard_map/all_to_all | solution.py:133
  300.5 0.5 copy.88
  301.1 6.8 stack.2
  307.9 162.9 %all_to_all.19 = bf16[16,8,1,9,6144]{4,1,3,2,0:T(8,128)(2,1)S(1)} all-to-all(bf16[16,8,1,9,6144]{4,1,3,2,0:T(8,128)(2,1)} %stack.2), channel_id=1, replica_groups=mesh['ctx'=16,'exp'=8] {'ctx'}, dimensions={0} | all-to-all | bytes 28311552 | tf_op jit(solution)/shard_map/all_to_all | solution.py:135
  470.8 5.1 copy-done.2
  475.9 17.1 %fusion = f32[128,9,576]{0,2,1:T(8,128)} fusion(bf16[16,8,1,9,6144]{4,1,3,2,0:T(8,128)(2,1)S(1)} %all_to_all.19, bf16[1,6144,576]{1,2,0:T(8,128)(2,1)} %param.28), kind=kOutput, calls=%fused_computation.2 | convolution fusion | flops 8153726976 | bytes 23887872 | tf_op jit(solution)/shard_map/nemd,edh->nemh/dot_general | solution.py:138
  493.0 32.2 %convert_bitcast_fusion = bf16[128,1,9,6144]{3,0,2,1:T(8,128)(2,1)} fusion(bf16[1,576,6144]{2,1,0:T(8,128)(2,1)} %param.29, f32[128,9,576]{0,2,1:T(8,128)} %fusion, bf16[1,6144,576]{1,2,0:T(8,128)(2,1)} %param.27, bf16[16,8,1,9,6144]{4,1,3,2,0:T(8,128)(2,1)} %copy-done.2), kind=kOutput, calls=%fused_computation.6 | convolution fusion | flops 16318513152 | bytes 45121536 | tf_op jit(solution)/shard_map/nemh,ehd->nemd/dot_general | solution.py:142
  526.0 190.2 %all-reduce.4.cloned.1.call-done = bf16[128,1,9,6144]{3,0,2,1:T(8,128)(2,1)} async-done(((bf16[128,1,9,6144]{3,0,2,1:T(8,128)(2,1)}), bf16[128,1,9,6144]{3,0,2,1:T(8,128)(2,1)}) %all-reduce.4.cloned.1.call-update) | async-done | bytes 14155792
  716.2 1.2 constant_dynamic-slice_fusion
  717.5 1.7 copy.90
  719.2 5.1 all-to-all-start.2
  724.3 0.1 sub.41
  724.4 0.1 copy.86
  724.4 0.1 select_reduce_fusion
  724.5 20.4 %all-to-all-done.2 = bf16[8,1,9,6144]{3,2,1,0:T(8,128)(2,1)S(1)} async-done(((bf16[8,1,9,6144]{3,2,1,0:T(8,128)(2,1)}), bf16[8,1,9,6144]{3,2,1,0:T(8,128)(2,1)S(1)}, u32[]{:S(2)}, u32[]{:S(2)}) %all-to-all-start.2) | async-done | bytes 884768 | tf_op jit(solution)/shard_map/all_to_all | solution.py:149
  745.0 0.4 reshape.185
  745.4 2.3 fusion.10
  (38 shorter events, 0.5 us)
Async XLA Ops:
  6.5 1.1 copy-start
  6.5 119.7 %all-gather.7.cloned.1.call-start = ((), (), s32[]{:S(2)}) async-start(), calls=%async_computation.6 | async-start | bytes 17825792 | tf_op jit(solution)/shard_map/all_gather | solution.py:10
  11.6 215.1 %all-gather.5.cloned.1.call-start = ((), (), s32[]{:S(2)}) async-start(), calls=%async_computation.4 | async-start | bytes 13369344 | tf_op jit(solution)/shard_map/all_gather | solution.py:106
  12.4 257.0 %reduce-scatter.3.cloned.1.call-start = ((), (), s32[]{:S(2)}) async-start(), calls=%async_computation.5 | async-start | bytes 3538944 | tf_op jit(solution)/shard_map/reduce_scatter | solution.py:108
  126.4 3.2 copy-start.4
  126.5 5.4 copy-start.6
  226.7 9.5 %copy-start.7 = (s32[1,32,2]{1,2,0:T(2,128)S(1)}, s32[1,32,2]{1,2,0:T(2,128)}, u32[]{:S(2)}) copy-start(s32[1,32,2]{1,2,0:T(2,128)} %param.25) | copy-start | bytes 772
  226.7 42.6 %copy-start.3 = (bf16[4,8,6144]{2,1,0:T(8,128)(2,1)S(1)}, bf16[4,8,6144]{2,1,0:T(8,128)(2,1)}, u32[]{:S(2)}) copy-start(bf16[4,8,6144]{2,1,0:T(8,128)(2,1)} %param.23) | copy-start | bytes 1179652
  226.7 43.8 %copy-start.5 = (f32[6144]{0:T(1024)S(1)}, f32[6144]{0:T(1024)}, u32[]{:S(2)}) copy-start(f32[6144]{0:T(1024)} %param.24) | copy-start | bytes 73732
  236.2 480.1 %all-reduce.4.cloned.1.call-start = ((), (), s32[]{:S(2)}) async-start(), calls=%async_computation.7 | async-start | bytes 28311552
  470.8 5.1 copy-start.2
  525.3 199.2 %copy-start.8 = (f32[1,32,2]{1,2,0:T(2,128)S(1)}, f32[1,32,2]{1,2,0:T(2,128)}, u32[]{:S(2)}) copy-start(f32[1,32,2]{1,2,0:T(2,128)} %param.26) | copy-start | bytes 772
  525.3 222.4 %copy-start.1 = (bf16[4,64,1024]{2,1,0:T(8,128)(2,1)S(1)}, bf16[4,64,1024]{2,1,0:T(8,128)(2,1)}, u32[]{:S(2)}) copy-start(bf16[4,64,1024]{2,1,0:T(8,128)(2,1)} %param.18) | copy-start | bytes 1572868
  719.2 25.8 %all-to-all-start.2 = ((bf16[8,1,9,6144]{3,2,1,0:T(8,128)(2,1)}), bf16[8,1,9,6144]{3,2,1,0:T(8,128)(2,1)S(1)}, u32[]{:S(2)}, u32[]{:S(2)}) async-start(bf16[8,1,9,6144]{3,2,1,0:T(8,128)(2,1)} %copy.90), calls=%async_computation.3 | async-start | bytes 3145728 | tf_op jit(solution)/shard_map/all_to_all | solution.py:149
Sparse Core Ops, SparseCore 0:
  11.7 114.4 all-gather.6
  128.3 98.3 all-gather.4
  236.3 32.9 reduce-scatter.2
  525.4 190.8 all-reduce.3
